TPU v7x, 256 devices: a whole 4x4x8 slice. The times are simulated.
256 devices in a mesh: cells: 16 (over z_hi, x, core), modes: 16 (over y, z_lo).
Axes of the slice: x: 4, y: 4, z: 8 (z_hi: 2, z_lo: 4; z = z_hi * 4 + z_lo), core: 2. Of those that a mesh axis runs over, the one named last changes fastest.
Arguments:
- hermite_coefficient_array: float32 [32, 64, 32, 2048], P('cells', None, None, 'modes'), may hold values from -6 to 6
- encounter_kernel_array: bfloat16 [14400, 120], replicated, may hold values from -0.046875 to 0.046875
- obstacle_indicator: int32 [32, 64, 32], P('cells'), may hold values 0 or 1
Outputs:
- moments_next: float32 [32, 64, 32, 2048], P('cells', None, None, 'modes')
All inputs are finite; a program needn't handle non-finite values. No bound on the sum of `obstacle_indicator` on one device may be relied on, other than what follows from the above.
Results may differ from a plain program's by a relative error of at most 0.0003.
Values sent between devices are 32-bit elements; how exact they have to be, the bound alone decides.
No kernel may reach another device: no remote copies, remote signals or barrier semaphores. Data moves between devices by JAX's collectives and lax.ppermute only.
A program may use at most 64 MiB of HBM per device.

v0:
```python
import math
import jax
import jax.numpy as jnp
from jax import lax
from jax.sharding import PartitionSpec as P

MA = 16
MB = 16
MC = 8
LDEG = 7
BASIS_SIZE = 120
MODES = 2048
CFL = 0.04
DTC = 0.2
PRECISE = lax.Precision.HIGHEST


def passed_along(shard, axis, by):
    length = lax.axis_size(axis)
    pairs = [(i, i + by) for i in range(length) if 0 <= i + by < length]
    return lax.ppermute(shard, axis, pairs)


def extended(cells, sides, width):
    for axis, dim in sides:
        count = lax.axis_size(axis)
        head = lax.slice_in_dim(cells, 0, width, axis=dim)
        tail = lax.slice_in_dim(cells, cells.shape[dim] - width, cells.shape[dim], axis=dim)
        cells = jnp.concatenate(
            [
                lax.ppermute(tail, axis, [(i, (i + 1) % count) for i in range(count)]),
                cells,
                lax.ppermute(head, axis, [((i + 1) % count, i) for i in range(count)]),
            ],
            axis=dim,
        )
    return cells


def digits(mode_index):
    digit_a = mode_index // (MB * MC)
    digit_b = mode_index // MC % MB
    digit_c = mode_index % MC
    return (digit_a, digit_b, digit_c)


def ladder(source, target, same_rest):
    level = target.astype(jnp.float32)
    down_term = jnp.where(same_rest & (source == target - 1), jnp.sqrt(level), 0.0)
    up_term = jnp.where(same_rest & (source == target + 1), jnp.sqrt(level + 1.0), 0.0)
    return down_term + up_term


def coupling(first_mode, local_modes):
    mode_index = first_mode + jnp.arange(local_modes, dtype=jnp.int32)
    source_a, source_b, source_c = digits(mode_index[:, None])
    target_a, target_b, target_c = digits(mode_index[None, :])
    same_a = source_a == target_a
    same_b = source_b == target_b
    same_c = source_c == target_c
    x_matrix = ladder(source_a, target_a, same_b & same_c)
    y_matrix = ladder(source_b, target_b, same_a & same_c)
    z_matrix = ladder(source_c, target_c, same_a & same_b)
    return (x_matrix, jnp.concatenate([y_matrix, z_matrix], 0))


def body(hermite_coefficient_array, encounter_kernel_array, obstacle_indicator):
    plane_count, rows_y, rows_z, local_modes = hermite_coefficient_array.shape
    block_size = MB * MC
    speed_x = 2.0 * math.sqrt(MA)
    speed_y = 2.0 * math.sqrt(MB)
    speed_z = 2.0 * math.sqrt(MC)
    all_index = jnp.arange(MODES, dtype=jnp.int32)
    all_a, all_b, all_c = digits(all_index)
    low_flags = (all_a + all_b + all_c <= LDEG).astype(jnp.int32)
    rank_all = jnp.cumsum(low_flags) - 1
    targets = jnp.arange(BASIS_SIZE, dtype=jnp.int32)
    first_mode = lax.axis_index("modes") * local_modes
    first_a = (first_mode // block_size).astype(jnp.float32)
    last_a = first_a + float(local_modes // block_size - 1)
    x_matrix, yz_matrix = coupling(first_mode, local_modes)
    full_matrix = jnp.concatenate([x_matrix, yz_matrix], 0)

    def across(first_axis_gradient):
        from_lower = passed_along(first_axis_gradient, "modes", 1)
        from_upper = passed_along(first_axis_gradient, "modes", -1)
        lower_term = jnp.sqrt(first_a) * from_lower
        upper_term = jnp.sqrt(last_a + 1.0) * from_upper
        return lower_term + upper_term

    def substep(center, behind, beyond, solid):
        first_axis_gradient = beyond - behind
        lap_x = beyond - 2.0 * center + behind
        next_y = jnp.roll(center, -1, 1)
        prev_y = jnp.roll(center, 1, 1)
        next_z = jnp.roll(center, -1, 2)
        prev_z = jnp.roll(center, 1, 2)
        diff_y = next_y - prev_y
        lap_y = next_y - 2.0 * center + prev_y
        diff_z = next_z - prev_z
        lap_z = next_z - 2.0 * center + prev_z
        flux = jnp.dot(
            jnp.concatenate([first_axis_gradient, diff_y, diff_z], -1),
            full_matrix,
            precision=PRECISE,
            preferred_element_type=jnp.float32,
        )
        flux = flux + across(first_axis_gradient)
        update = center + CFL * (
            -0.5 * flux + 0.5 * (speed_x * lap_x + speed_y * lap_y + speed_z * lap_z)
        )
        return jnp.where(solid[..., None] != 0, center, update)

    def widen(field):
        return extended(field, (("cells", 0),), 1)

    padded = widen(hermite_coefficient_array)
    middle = substep(hermite_coefficient_array, padded[:-2], padded[2:], obstacle_indicator)
    padded = widen(middle)
    transported = substep(middle, padded[:-2], padded[2:], obstacle_indicator)
    cell_count = plane_count * rows_y * rows_z
    rows = transported.reshape(cell_count, local_modes)
    local_flags = lax.dynamic_slice_in_dim(low_flags, first_mode, local_modes)
    local_rank = lax.dynamic_slice_in_dim(rank_all, first_mode, local_modes)
    selector = ((local_flags[:, None] == 1) & (local_rank[:, None] == targets[None, :])).astype(
        jnp.float32
    )
    share_rows = cell_count // lax.axis_size("modes")
    low = lax.psum_scatter(
        jnp.dot(rows, selector, precision=PRECISE, preferred_element_type=jnp.float32),
        "modes",
        scatter_dimension=0,
        tiled=True,
    )
    quadratic_factors = (
        (low[:, :, None] * low[:, None, :])
        .reshape(share_rows, BASIS_SIZE * BASIS_SIZE)
        .astype(jnp.bfloat16)
    )
    scattered_state = jnp.dot(
        quadratic_factors, encounter_kernel_array, preferred_element_type=jnp.float32
    )
    lifted = jnp.dot(
        lax.all_gather(scattered_state, "modes", axis=0, tiled=True),
        selector.T,
        precision=PRECISE,
        preferred_element_type=jnp.float32,
    )
    result = rows + DTC * lifted
    return result.reshape(plane_count, rows_y, rows_z, local_modes)


def solution(mesh):
    placed = (P("cells", None, None, "modes"), P(), P("cells", None, None))
    return jax.shard_map(
        body, mesh=mesh, in_specs=placed, out_specs=P("cells", None, None, "modes"), check_vma=False
    )
```

profile of v0, /device:TPU:6, one launch (start us, length us, event | category | flops | bytes accessed | tf_op | source)
XLA Modules:
  0.0 488.2 jit_solution(3035547686091999700)
XLA Ops:
  6.5 3.2 fusion.65
  9.7 1.7 collective-permute-start
  11.6 0.7 copy.7
  12.4 11.9 %collective-permute-done.1 = f32[1,64,32,128]{3,2,1,0:T(8,128)} collective-permute-done((f32[1,64,32,128]{3,2,1,0:T(8,128)}, f32[1,64,32,128]{3,2,1,0:T(8,128)}, u32[]{:S(2)}, u32[]{:S(2)}) %collective-permute-start.1) | collective-permute-done | bytes 1048608 | tf_op jit(solution)/shard_map/ppermute | solution.py:31
  24.3 2.7 fusion.23
  26.9 1.3 collective-permute-start.3
  28.2 4.7 collective-permute-start.2
  33.7 0.7 fusion.61
  34.4 1.1 fusion.16
  35.5 0.8 select_add_fusion.2
  36.3 35.2 %collective-permute-done.3 = f32[2,64,32,128]{3,2,1,0:T(8,128)S(1)} collective-permute-done((f32[2,64,32,128]{3,2,1,0:T(8,128)S(1)}, f32[2,64,32,128]{3,2,1,0:T(8,128)S(1)}, u32[]{:S(2)}, u32[]{:S(2)}) %collective-permute-start.3) | collective-permute-done | bytes 2097184 | tf_op jit(solution)/shard_map/ppermute | solution.py:21
  71.5 1.3 copy-done.8
  72.8 0.7 copy-done.9
  73.5 9.4 %add_select_fusion.1 = f32[2,64,32,128]{3,2,1,0:T(8,128)S(1)} fusion(f32[2,64,32,128]{3,2,1,0:T(8,128)S(1)} %copy-done.1, f32[2,64,32,128]{3,2,1,0:T(8,128)} %copy-done.8, f32[2,64,32,128]{3,2,1,0:T(8,128)} %copy-done.9, f32[2,63,32,128]{3,2,1,0:T(8,128)S(1)} %get-tuple-element.20, f32[2,1,32,128]{3,2,1,0:T(8,128)S(1)} %get-tuple-element.22, ...), kind=kOutput, calls=%fused_computation.16 | convolution fusion | flops 2433318912 | bytes 25366536 | tf_op jit(solution)/shard_map/dot_general | solution.py:102
  82.9 1.6 fusion.60
  84.9 59.8 %collective-permute-start.5 = (f32[1,64,32,128]{3,2,1,0:T(8,128)}, f32[1,64,32,128]{3,2,1,0:T(8,128)}, u32[]{:S(2)}, u32[]{:S(2)}) collective-permute-start(f32[1,64,32,128]{3,2,1,0:T(8,128)} %get-tuple-element.13), channel_id=1, source_target_pairs={{0,16},{16,32},{32,48},{48,64},{64,80},{80,96},{96,112},{112,128},... | collective-permute-start | bytes 3145736 | tf_op jit(solution)/shard_map/ppermute | solution.py:31
  145.7 0.8 slice_reduce_fusion
  147.3 10.0 %collective-permute-done.4 = f32[1,64,32,128]{3,2,1,0:T(8,128)} collective-permute-done((f32[1,64,32,128]{3,2,1,0:T(8,128)}, f32[1,64,32,128]{3,2,1,0:T(8,128)}, u32[]{:S(2)}, u32[]{:S(2)}) %collective-permute-start.4) | collective-permute-done | bytes 1048608 | tf_op jit(solution)/shard_map/ppermute | solution.py:33
  157.3 2.6 fusion.24
  160.0 1.3 collective-permute-start.7
  161.3 5.9 %collective-permute-start.6 = (f32[2,64,32,128]{3,2,1,0:T(8,128)S(1)}, f32[2,64,32,128]{3,2,1,0:T(8,128)}, u32[]{:S(2)}, u32[]{:S(2)}) collective-permute-start(f32[2,64,32,128]{3,2,1,0:T(8,128)S(1)} %fusion.24), channel_id=1, source_target_pairs={{0,1},{1,2},{2,3},{3,4},{4,5},{5,6},{6,7},{7,8},{8,9},{9,10},{10,1... | collective-permute-start | bytes 6291464 | tf_op jit(solution)/shard_map/ppermute | solution.py:21
  168.5 0.7 fusion.56
  169.7 52.6 %collective-permute-done.7 = f32[2,64,32,128]{3,2,1,0:T(8,128)S(1)} collective-permute-done((f32[2,64,32,128]{3,2,1,0:T(8,128)S(1)}, f32[2,64,32,128]{3,2,1,0:T(8,128)S(1)}, u32[]{:S(2)}, u32[]{:S(2)}) %collective-permute-start.7) | collective-permute-done | bytes 2097184 | tf_op jit(solution)/shard_map/ppermute | solution.py:21
  222.4 1.3 copy-done.10
  223.7 9.4 %add_select_fusion = f32[2,64,32,128]{3,2,1,0:T(8,128)S(1)} fusion(f32[2,64,32,128]{3,2,1,0:T(8,128)S(1)} %copy-done.3, f32[2,64,32,128]{3,2,1,0:T(8,128)} %copy-done.10, f32[2,64,32,128]{3,2,1,0:T(8,128)} %collective-permute-done.6, f32[2,63,32,128]{3,2,1,0:T(8,128)S(1)} %get-tuple-element.10, f32[2,1,32,128]{3,2,1,0:T(8,128)S(1)} %get-tuple-element.12, ...), kind=kOutput, calls=%fused_computation.15 | convolution fusion | flops 2433318912 | bytes 25366536 | tf_op jit(solution)/shard_map/dot_general | solution.py:102
  233.1 1.3 copy-done.4
  234.4 2.5 fusion.27
  237.0 149.5 %reduce-scatter.2.cloned.1.call-done = f32[256,120]{0,1:T(8,128)} async-done(((f32[4096,120]{0,1:T(8,128)}), f32[256,120]{0,1:T(8,128)}) %reduce-scatter.2.cloned.1.call-update) | async-done | bytes 122896 | tf_op jit(solution)/shard_map/reduce_scatter | solution.py:129
  386.5 3.7 multiply_convert_fusion
  390.3 2.8 fusion.66
  393.1 83.6 %all-gather.2.cloned.1.call-done = f32[4096,120]{1,0:T(8,128)} async-done(((f32[256,120]{1,0:T(8,128)}), f32[4096,120]{1,0:T(8,128)}) %all-gather.2.cloned.1.call-update) | async-done | bytes 1966096 | tf_op jit(solution)/shard_map/all_gather | solution.py:144
  476.6 4.7 fusion.12
  (57 shorter events, 5.0 us)
Async XLA Ops:
  6.5 383.7 %copy-start = (bf16[14400,120]{0,1:T(8,128)(2,1)S(1)}, bf16[14400,120]{0,1:T(8,128)(2,1)}, u32[]{:S(2)}) copy-start(bf16[14400,120]{0,1:T(8,128)(2,1)} %param.4) | copy-start | bytes 10368004
  6.5 5.0 %copy-start.5 = (s32[2,64,32]{1,2,0:T(8,128)S(1)}, s32[2,64,32]{1,2,0:T(8,128)}, u32[]{:S(2)}) copy-start(s32[2,64,32]{1,2,0:T(8,128)} %param.5) | copy-start | bytes 49156
  6.5 380.0 %reduce-scatter.2.cloned.1.call-start = ((), (), s32[]{:S(2)}) async-start(), calls=%async_computation.1 | async-start | bytes 2088960 | tf_op jit(solution)/shard_map/reduce_scatter | solution.py:129
  9.7 14.5 %collective-permute-start.1 = (f32[1,64,32,128]{3,2,1,0:T(8,128)}, f32[1,64,32,128]{3,2,1,0:T(8,128)}, u32[]{:S(2)}, u32[]{:S(2)}) collective-permute-start(f32[1,64,32,128]{3,2,1,0:T(8,128)} %get-tuple-element.23), channel_id=1, source_target_pairs={{0,16},{16,32},{32,48},{48,64},{64,80},{80,96},{96,112},{112,128},... | collective-permute-start | bytes 3145736 | tf_op jit(solution)/shard_map/ppermute | solution.py:31
  9.7 14.5 %collective-permute-start = (f32[1,64,32,128]{3,2,1,0:T(8,128)}, f32[1,64,32,128]{3,2,1,0:T(8,128)}, u32[]{:S(2)}, u32[]{:S(2)}) collective-permute-start(f32[1,64,32,128]{3,2,1,0:T(8,128)} %get-tuple-element.24), channel_id=1, source_target_pairs={{16,0},{32,16},{48,32},{64,48},{80,64},{96,80},{112,96},{128,112},... | collective-permute-start | bytes 3145736 | tf_op jit(solution)/shard_map/ppermute | solution.py:33
  12.4 20.6 %copy-start.1 = (f32[2,64,32,128]{3,2,1,0:T(8,128)S(1)}, f32[2,64,32,128]{3,2,1,0:T(8,128)}, u32[]{:S(2)}) copy-start(f32[2,64,32,128]{3,2,1,0:T(8,128)} %param.3) | copy-start | bytes 6291460
  26.9 44.5 %collective-permute-start.3 = (f32[2,64,32,128]{3,2,1,0:T(8,128)S(1)}, f32[2,64,32,128]{3,2,1,0:T(8,128)S(1)}, u32[]{:S(2)}, u32[]{:S(2)}) collective-permute-start(f32[2,64,32,128]{3,2,1,0:T(8,128)S(1)} %fusion.23), channel_id=1, source_target_pairs={{1,0},{2,1},{3,2},{4,3},{5,4},{6,5},{7,6},{8,7},{9,8},{10,9},{11,1... | collective-permute-start | bytes 6291464 | tf_op jit(solution)/shard_map/ppermute | solution.py:21
  28.2 43.2 %collective-permute-start.2 = (f32[2,64,32,128]{3,2,1,0:T(8,128)S(1)}, f32[2,64,32,128]{3,2,1,0:T(8,128)S(1)}, u32[]{:S(2)}, u32[]{:S(2)}) collective-permute-start(f32[2,64,32,128]{3,2,1,0:T(8,128)S(1)} %fusion.23), channel_id=1, source_target_pairs={{0,1},{1,2},{2,3},{3,4},{4,5},{5,6},{6,7},{7,8},{8,9},{9,10},{10,1... | collective-permute-start | bytes 6291464 | tf_op jit(solution)/shard_map/ppermute | solution.py:21
  34.4 39.1 %copy-start.6 = (pred[2,64,32]{2,1,0:T(8,128)(4,1)S(1)}, pred[2,64,32]{2,1,0:T(8,128)(4,1)}, u32[]{:S(2)}) copy-start(pred[2,64,32]{2,1,0:T(8,128)(4,1)} %copy.7) | copy-start | bytes 12292
  71.4 1.3 copy-start.8
  71.4 2.0 copy-start.9
  82.9 2.0 copy-start.2
  84.9 62.4 %collective-permute-start.5 = (f32[1,64,32,128]{3,2,1,0:T(8,128)}, f32[1,64,32,128]{3,2,1,0:T(8,128)}, u32[]{:S(2)}, u32[]{:S(2)}) collective-permute-start(f32[1,64,32,128]{3,2,1,0:T(8,128)} %get-tuple-element.13), channel_id=1, source_target_pairs={{0,16},{16,32},{32,48},{48,64},{64,80},{80,96},{96,112},{112,128},... | collective-permute-start | bytes 3145736 | tf_op jit(solution)/shard_map/ppermute | solution.py:31
  144.7 12.6 %collective-permute-start.4 = (f32[1,64,32,128]{3,2,1,0:T(8,128)}, f32[1,64,32,128]{3,2,1,0:T(8,128)}, u32[]{:S(2)}, u32[]{:S(2)}) collective-permute-start(f32[1,64,32,128]{3,2,1,0:T(8,128)} %get-tuple-element.14), channel_id=1, source_target_pairs={{16,0},{32,16},{48,32},{64,48},{80,64},{96,80},{112,96},{128,112},... | collective-permute-start | bytes 3145736 | tf_op jit(solution)/shard_map/ppermute | solution.py:33
  146.7 20.6 %copy-start.3 = (f32[2,64,32,128]{3,2,1,0:T(8,128)S(1)}, f32[2,64,32,128]{3,2,1,0:T(8,128)}, u32[]{:S(2)}) copy-start(f32[2,64,32,128]{3,2,1,0:T(8,128)} %copy-done.2) | copy-start | bytes 6291460
  160.0 62.4 %collective-permute-start.7 = (f32[2,64,32,128]{3,2,1,0:T(8,128)S(1)}, f32[2,64,32,128]{3,2,1,0:T(8,128)S(1)}, u32[]{:S(2)}, u32[]{:S(2)}) collective-permute-start(f32[2,64,32,128]{3,2,1,0:T(8,128)S(1)} %fusion.24), channel_id=1, source_target_pairs={{1,0},{2,1},{3,2},{4,3},{5,4},{6,5},{7,6},{8,7},{9,8},{10,9},{11,1... | collective-permute-start | bytes 6291464 | tf_op jit(solution)/shard_map/ppermute | solution.py:21
  161.3 62.4 %collective-permute-start.6 = (f32[2,64,32,128]{3,2,1,0:T(8,128)S(1)}, f32[2,64,32,128]{3,2,1,0:T(8,128)}, u32[]{:S(2)}, u32[]{:S(2)}) collective-permute-start(f32[2,64,32,128]{3,2,1,0:T(8,128)S(1)} %fusion.24), channel_id=1, source_target_pairs={{0,1},{1,2},{2,3},{3,4},{4,5},{5,6},{6,7},{7,8},{8,9},{9,10},{10,1... | collective-permute-start | bytes 6291464 | tf_op jit(solution)/shard_map/ppermute | solution.py:21
  169.2 54.5 %copy-start.7 = (pred[2,64,32]{2,1,0:T(8,128)(4,1)S(1)}, pred[2,64,32]{2,1,0:T(8,128)(4,1)}, u32[]{:S(2)}) copy-start(pred[2,64,32]{2,1,0:T(8,128)(4,1)} %copy.7) | copy-start | bytes 12292
  222.4 1.3 copy-start.10
  233.1 1.3 copy-start.4
  237.0 239.6 %all-gather.2.cloned.1.call-start = ((), (), s32[]{:S(2)}) async-start(), calls=%async_computation.2 | async-start | bytes 2228224 | tf_op jit(solution)/shard_map/all_gather | solution.py:144
Sparse Core Ops, SparseCore 0:
  237.1 149.3 reduce-scatter.1
  393.2 83.3 all-gather.1
where the time goes:
time: 488 us
  waiting for transfers between devices  343 us (70%)
  starting transfers between devices  74.7 us (15%)
  matrix products  28.8 us (6%)
  local copies, waits for them, and re-layouts  14.2 us (3%)
  between operations  13.8 us (3%)
  other arithmetic  13.3 us (3%)
    reduce_scatter x1, waiting for transfers between devices, body(): lax.psum_scatter(jnp.dot(rows, selector, precision=PRECISE, preferred_ele...  149 us
    ppermute x4, waiting for transfers between devices, passed_along(): return lax.ppermute(shard, axis, pairs)  87.8 us
    all_gather x1, waiting for transfers between devices, body(): lax.all_gather(scattered_state, 'modes', axis=0, tiled=True)  83.6 us
    ppermute x2, starting transfers between devices, extended(): lax.ppermute(tail, axis, [(i, (i + 1) % count) for i in range(count)])  59.8 us
    dot_general x2, matrix products, substep(): jnp.dot(jnp.concatenate([first_axis_gradient, diff_y, diff_z], -1), full_...  18.8 us
    ppermute x4, starting transfers between devices, passed_along(): return lax.ppermute(shard, axis, pairs)  13.2 us
    ppermute x2, waiting for transfers between devices, extended(): lax.ppermute(tail, axis, [(i, (i + 1) % count) for i in range(count)])  12.5 us
    ppermute x2, waiting for transfers between devices, extended(): lax.ppermute(head, axis, [((i + 1) % count, i) for i in range(count)])  10 us
  transfers between devices with their start and end apart: 10, of which 7 were waited for; matrix products, arithmetic and copies ran while one was open for 2% of the time, Pallas kernels for 0%

commit v1 on v0

--- a/solution.py
+++ b/solution.py
@@ -141,7 +141,10 @@
         quadratic_factors, encounter_kernel_array, preferred_element_type=jnp.float32
     )
     lifted = jnp.dot(
-        lax.all_gather(scattered_state, "modes", axis=0, tiled=True),
+        jnp.concatenate(
+            lax.all_to_all(jnp.stack([scattered_state] * lax.axis_size("modes")), "modes", 0, 0),
+            axis=0,
+        ),
         selector.T,
         precision=PRECISE,
         preferred_element_type=jnp.float32,

time: 488 us -> 444 us (0.910)
  waiting for transfers between devices: 343 us -> 260 us
  blocking collectives: 0 us -> 40.4 us
    all_gather x1 -> x0, waiting for transfers between devices: 83.6 us -> none  [body(): lax.all_gather(scattered_state, 'modes', axis=0, tiled=True)]
    all_to_all x0 -> x1, blocking collectives: none -> 40.4 us  [body(): lax.all_to_all(jnp.stack([scattered_state] * lax.axis_size('modes')), 'mo...]
  transfers between devices with their start and end apart: 10 -> 9, of which waited for: 7 -> 6; matrix products, arithmetic and copies ran while one was open for 2% -> 2% of each run, Pallas kernels for 0% -> 0%
where the time goes in v1:
time: 444 us; the launch traced here: 443 us
  waiting for transfers between devices  260 us (59%)
  starting transfers between devices  74.7 us (17%)
  blocking collectives  40.4 us (9%)
  matrix products  25.7 us (6%)
  local copies, waits for them, and re-layouts  15.3 us (3%)
  between operations  13.8 us (3%)
  other arithmetic  13.3 us (3%)
    reduce_scatter x1, waiting for transfers between devices, body(): lax.psum_scatter(jnp.dot(rows, selector, precision=PRECISE, preferred_ele...  149 us
    ppermute x4, waiting for transfers between devices, passed_along(): return lax.ppermute(shard, axis, pairs)  87.8 us
    ppermute x2, starting transfers between devices, extended(): lax.ppermute(tail, axis, [(i, (i + 1) % count) for i in range(count)])  59.8 us
    all_to_all x1, blocking collectives, body(): lax.all_to_all(jnp.stack([scattered_state] * lax.axis_size('modes')), 'mo...  40.4 us
    dot_general x2, matrix products, substep(): jnp.dot(jnp.concatenate([first_axis_gradient, diff_y, diff_z], -1), full_...  18.8 us
    ppermute x4, starting transfers between devices, passed_along(): return lax.ppermute(shard, axis, pairs)  13.2 us
    ppermute x2, waiting for transfers between devices, extended(): lax.ppermute(tail, axis, [(i, (i + 1) % count) for i in range(count)])  13.1 us
    ppermute x2, waiting for transfers between devices, extended(): lax.ppermute(head, axis, [((i + 1) % count, i) for i in range(count)])  10 us
  transfers between devices with their start and end apart: 9, of which 6 were waited for; matrix products, arithmetic and copies ran while one was open for 2% of the time, Pallas kernels for 0%

profile of v1, /device:TPU:6, one launch (start us, length us, event | category | flops | bytes accessed | tf_op | source)
XLA Modules:
  0.0 443.4 jit_solution(12569997891433344468)
XLA Ops:
  6.5 3.2 fusion.65
  9.7 1.7 collective-permute-start
  11.8 12.5 %collective-permute-done.1 = f32[1,64,32,128]{3,2,1,0:T(8,128)} collective-permute-done((f32[1,64,32,128]{3,2,1,0:T(8,128)}, f32[1,64,32,128]{3,2,1,0:T(8,128)}, u32[]{:S(2)}, u32[]{:S(2)}) %collective-permute-start.1) | collective-permute-done | bytes 1048608 | tf_op jit(solution)/shard_map/ppermute | solution.py:31
  24.3 2.7 fusion.23
  26.9 1.3 collective-permute-start.3
  28.2 4.7 %collective-permute-start.2 = (f32[2,64,32,128]{3,2,1,0:T(8,128)S(1)}, f32[2,64,32,128]{3,2,1,0:T(8,128)S(1)}, u32[]{:S(2)}, u32[]{:S(2)}) collective-permute-start(f32[2,64,32,128]{3,2,1,0:T(8,128)S(1)} %fusion.23), channel_id=1, source_target_pairs={{0,1},{1,2},{2,3},{3,4},{4,5},{5,6},{6,7},{7,8},{8,9},{9,10},{10,1... | collective-permute-start | bytes 6291464 | tf_op jit(solution)/shard_map/ppermute | solution.py:21
  33.7 0.7 fusion.61
  34.4 1.1 fusion.16
  35.5 0.8 select_add_fusion.2
  36.3 35.1 %collective-permute-done.3 = f32[2,64,32,128]{3,2,1,0:T(8,128)S(1)} collective-permute-done((f32[2,64,32,128]{3,2,1,0:T(8,128)S(1)}, f32[2,64,32,128]{3,2,1,0:T(8,128)S(1)}, u32[]{:S(2)}, u32[]{:S(2)}) %collective-permute-start.3) | collective-permute-done | bytes 2097184 | tf_op jit(solution)/shard_map/ppermute | solution.py:21
  71.4 1.3 copy-done.9
  72.8 0.7 copy-done.10
  73.5 9.4 %add_select_fusion.1 = f32[2,64,32,128]{3,2,1,0:T(8,128)S(1)} fusion(f32[2,64,32,128]{3,2,1,0:T(8,128)S(1)} %copy-done.1, f32[2,64,32,128]{3,2,1,0:T(8,128)} %copy-done.9, f32[2,64,32,128]{3,2,1,0:T(8,128)} %copy-done.10, f32[2,63,32,128]{3,2,1,0:T(8,128)S(1)} %get-tuple-element.20, f32[2,1,32,128]{3,2,1,0:T(8,128)S(1)} %get-tuple-element.22, ...), kind=kOutput, calls=%fused_computation.16 | convolution fusion | flops 2433318912 | bytes 25366536 | tf_op jit(solution)/shard_map/dot_general | solution.py:102
  82.9 1.6 fusion.60
  84.9 59.8 %collective-permute-start.5 = (f32[1,64,32,128]{3,2,1,0:T(8,128)}, f32[1,64,32,128]{3,2,1,0:T(8,128)}, u32[]{:S(2)}, u32[]{:S(2)}) collective-permute-start(f32[1,64,32,128]{3,2,1,0:T(8,128)} %get-tuple-element.13), channel_id=1, source_target_pairs={{0,16},{16,32},{32,48},{48,64},{64,80},{80,96},{96,112},{112,128},... | collective-permute-start | bytes 3145736 | tf_op jit(solution)/shard_map/ppermute | solution.py:31
  145.7 0.8 slice_reduce_fusion
  147.3 10.0 %collective-permute-done.4 = f32[1,64,32,128]{3,2,1,0:T(8,128)} collective-permute-done((f32[1,64,32,128]{3,2,1,0:T(8,128)}, f32[1,64,32,128]{3,2,1,0:T(8,128)}, u32[]{:S(2)}, u32[]{:S(2)}) %collective-permute-start.4) | collective-permute-done | bytes 1048608 | tf_op jit(solution)/shard_map/ppermute | solution.py:33
  157.3 2.6 fusion.24
  160.0 1.3 collective-permute-start.7
  161.3 5.9 %collective-permute-start.6 = (f32[2,64,32,128]{3,2,1,0:T(8,128)S(1)}, f32[2,64,32,128]{3,2,1,0:T(8,128)}, u32[]{:S(2)}, u32[]{:S(2)}) collective-permute-start(f32[2,64,32,128]{3,2,1,0:T(8,128)S(1)} %fusion.24), channel_id=1, source_target_pairs={{0,1},{1,2},{2,3},{3,4},{4,5},{5,6},{6,7},{7,8},{8,9},{9,10},{10,1... | collective-permute-start | bytes 6291464 | tf_op jit(solution)/shard_map/ppermute | solution.py:21
  168.5 0.7 fusion.56
  169.8 52.6 %collective-permute-done.7 = f32[2,64,32,128]{3,2,1,0:T(8,128)S(1)} collective-permute-done((f32[2,64,32,128]{3,2,1,0:T(8,128)S(1)}, f32[2,64,32,128]{3,2,1,0:T(8,128)S(1)}, u32[]{:S(2)}, u32[]{:S(2)}) %collective-permute-start.7) | collective-permute-done | bytes 2097184 | tf_op jit(solution)/shard_map/ppermute | solution.py:21
  222.4 1.3 copy-done.11
  223.7 9.4 %add_select_fusion = f32[2,64,32,128]{3,2,1,0:T(8,128)S(1)} fusion(f32[2,64,32,128]{3,2,1,0:T(8,128)S(1)} %copy-done.3, f32[2,64,32,128]{3,2,1,0:T(8,128)} %copy-done.11, f32[2,64,32,128]{3,2,1,0:T(8,128)} %collective-permute-done.6, f32[2,63,32,128]{3,2,1,0:T(8,128)S(1)} %get-tuple-element.10, f32[2,1,32,128]{3,2,1,0:T(8,128)S(1)} %get-tuple-element.12, ...), kind=kOutput, calls=%fused_computation.15 | convolution fusion | flops 2433318912 | bytes 25366536 | tf_op jit(solution)/shard_map/dot_general | solution.py:102
  233.1 1.3 copy-done.4
  234.4 2.5 fusion.27
  237.0 149.4 %reduce-scatter.2.cloned.1.call-done = f32[256,120]{0,1:T(8,128)} async-done(((f32[4096,120]{0,1:T(8,128)}), f32[256,120]{0,1:T(8,128)}) %reduce-scatter.2.cloned.1.call-update) | async-done | bytes 122896 | tf_op jit(solution)/shard_map/reduce_scatter | solution.py:129
  386.4 3.7 multiply_convert_fusion
  390.1 1.1 fusion.66
  391.4 40.4 %all_to_all.5 = f32[16,256,120]{1,2,0:T(8,128)S(1)} all-to-all(f32[16,256,120]{1,2,0:T(8,128)S(1)} %stack.2), channel_id=1, replica_groups=mesh['cells'=16,'modes'=16] {'modes'}, dimensions={0} | all-to-all | bytes 3932160 | tf_op jit(solution)/shard_map/all_to_all | solution.py:145
  431.9 1.4 copy-done.5
  433.3 3.2 fusion.12
  (59 shorter events, 5.3 us)
Async XLA Ops:
  6.5 383.6 %copy-start = (bf16[14400,120]{0,1:T(8,128)(2,1)S(1)}, bf16[14400,120]{0,1:T(8,128)(2,1)}, u32[]{:S(2)}) copy-start(bf16[14400,120]{0,1:T(8,128)(2,1)} %param.4) | copy-start | bytes 10368004
  6.5 5.0 %copy-start.6 = (s32[2,64,32]{1,2,0:T(8,128)S(1)}, s32[2,64,32]{1,2,0:T(8,128)}, u32[]{:S(2)}) copy-start(s32[2,64,32]{1,2,0:T(8,128)} %param.5) | copy-start | bytes 49156
  6.5 379.8 %reduce-scatter.2.cloned.1.call-start = ((), (), s32[]{:S(2)}) async-start(), calls=%async_computation.2 | async-start | bytes 2088960 | tf_op jit(solution)/shard_map/reduce_scatter | solution.py:129
  9.7 14.5 %collective-permute-start.1 = (f32[1,64,32,128]{3,2,1,0:T(8,128)}, f32[1,64,32,128]{3,2,1,0:T(8,128)}, u32[]{:S(2)}, u32[]{:S(2)}) collective-permute-start(f32[1,64,32,128]{3,2,1,0:T(8,128)} %get-tuple-element.23), channel_id=1, source_target_pairs={{0,16},{16,32},{32,48},{48,64},{64,80},{80,96},{96,112},{112,128},... | collective-permute-start | bytes 3145736 | tf_op jit(solution)/shard_map/ppermute | solution.py:31
  9.7 14.5 %collective-permute-start = (f32[1,64,32,128]{3,2,1,0:T(8,128)}, f32[1,64,32,128]{3,2,1,0:T(8,128)}, u32[]{:S(2)}, u32[]{:S(2)}) collective-permute-start(f32[1,64,32,128]{3,2,1,0:T(8,128)} %get-tuple-element.24), channel_id=1, source_target_pairs={{16,0},{32,16},{48,32},{64,48},{80,64},{96,80},{112,96},{128,112},... | collective-permute-start | bytes 3145736 | tf_op jit(solution)/shard_map/ppermute | solution.py:33
  11.7 61.8 %copy-start.7 = (pred[2,64,32]{2,1,0:T(8,128)(4,1)}, pred[2,64,32]{2,1,0:T(8,128)(4,1)S(1)}, u32[]{:S(2)}) copy-start(pred[2,64,32]{2,1,0:T(8,128)(4,1)S(1)} %copy.11) | copy-start | bytes 12292
  11.8 21.2 %copy-start.1 = (f32[2,64,32,128]{3,2,1,0:T(8,128)S(1)}, f32[2,64,32,128]{3,2,1,0:T(8,128)}, u32[]{:S(2)}) copy-start(f32[2,64,32,128]{3,2,1,0:T(8,128)} %param.3) | copy-start | bytes 6291460
  26.9 44.5 %collective-permute-start.3 = (f32[2,64,32,128]{3,2,1,0:T(8,128)S(1)}, f32[2,64,32,128]{3,2,1,0:T(8,128)S(1)}, u32[]{:S(2)}, u32[]{:S(2)}) collective-permute-start(f32[2,64,32,128]{3,2,1,0:T(8,128)S(1)} %fusion.23), channel_id=1, source_target_pairs={{1,0},{2,1},{3,2},{4,3},{5,4},{6,5},{7,6},{8,7},{9,8},{10,9},{11,1... | collective-permute-start | bytes 6291464 | tf_op jit(solution)/shard_map/ppermute | solution.py:21
  28.2 43.2 %collective-permute-start.2 = (f32[2,64,32,128]{3,2,1,0:T(8,128)S(1)}, f32[2,64,32,128]{3,2,1,0:T(8,128)S(1)}, u32[]{:S(2)}, u32[]{:S(2)}) collective-permute-start(f32[2,64,32,128]{3,2,1,0:T(8,128)S(1)} %fusion.23), channel_id=1, source_target_pairs={{0,1},{1,2},{2,3},{3,4},{4,5},{5,6},{6,7},{7,8},{8,9},{9,10},{10,1... | collective-permute-start | bytes 6291464 | tf_op jit(solution)/shard_map/ppermute | solution.py:21
  71.4 1.3 copy-start.9
  71.4 2.0 copy-start.10
  82.9 2.0 copy-start.2
  84.9 62.4 %collective-permute-start.5 = (f32[1,64,32,128]{3,2,1,0:T(8,128)}, f32[1,64,32,128]{3,2,1,0:T(8,128)}, u32[]{:S(2)}, u32[]{:S(2)}) collective-permute-start(f32[1,64,32,128]{3,2,1,0:T(8,128)} %get-tuple-element.13), channel_id=1, source_target_pairs={{0,16},{16,32},{32,48},{48,64},{64,80},{80,96},{96,112},{112,128},... | collective-permute-start | bytes 3145736 | tf_op jit(solution)/shard_map/ppermute | solution.py:31
  144.7 12.6 %collective-permute-start.4 = (f32[1,64,32,128]{3,2,1,0:T(8,128)}, f32[1,64,32,128]{3,2,1,0:T(8,128)}, u32[]{:S(2)}, u32[]{:S(2)}) collective-permute-start(f32[1,64,32,128]{3,2,1,0:T(8,128)} %get-tuple-element.14), channel_id=1, source_target_pairs={{16,0},{32,16},{48,32},{64,48},{80,64},{96,80},{112,96},{128,112},... | collective-permute-start | bytes 3145736 | tf_op jit(solution)/shard_map/ppermute | solution.py:33
  146.7 20.7 %copy-start.3 = (f32[2,64,32,128]{3,2,1,0:T(8,128)S(1)}, f32[2,64,32,128]{3,2,1,0:T(8,128)}, u32[]{:S(2)}) copy-start(f32[2,64,32,128]{3,2,1,0:T(8,128)} %copy-done.2) | copy-start | bytes 6291460
  160.0 62.4 %collective-permute-start.7 = (f32[2,64,32,128]{3,2,1,0:T(8,128)S(1)}, f32[2,64,32,128]{3,2,1,0:T(8,128)S(1)}, u32[]{:S(2)}, u32[]{:S(2)}) collective-permute-start(f32[2,64,32,128]{3,2,1,0:T(8,128)S(1)} %fusion.24), channel_id=1, source_target_pairs={{1,0},{2,1},{3,2},{4,3},{5,4},{6,5},{7,6},{8,7},{9,8},{10,9},{11,1... | collective-permute-start | bytes 6291464 | tf_op jit(solution)/shard_map/ppermute | solution.py:21
  161.3 62.4 %collective-permute-start.6 = (f32[2,64,32,128]{3,2,1,0:T(8,128)S(1)}, f32[2,64,32,128]{3,2,1,0:T(8,128)}, u32[]{:S(2)}, u32[]{:S(2)}) collective-permute-start(f32[2,64,32,128]{3,2,1,0:T(8,128)S(1)} %fusion.24), channel_id=1, source_target_pairs={{0,1},{1,2},{2,3},{3,4},{4,5},{5,6},{6,7},{7,8},{8,9},{9,10},{10,1... | collective-permute-start | bytes 6291464 | tf_op jit(solution)/shard_map/ppermute | solution.py:21
  169.2 54.5 %copy-start.8 = (pred[2,64,32]{2,1,0:T(8,128)(4,1)S(1)}, pred[2,64,32]{2,1,0:T(8,128)(4,1)}, u32[]{:S(2)}) copy-start(pred[2,64,32]{2,1,0:T(8,128)(4,1)} %copy-done.7) | copy-start | bytes 12292
  222.4 1.3 copy-start.11
  233.1 1.3 copy-start.4
  431.7 1.6 copy-start.5
Sparse Core Ops, SparseCore 0:
  237.1 149.2 reduce-scatter.1
